TPU v7x, 32 devices: a whole 2x2x4 slice. The times are simulated.
32 devices in a mesh: grp: 2 (over x), seq: 16 (over z, y, core).
Axes of the slice: x: 2, y: 2, z: 4, core: 2. Of those that a mesh axis runs over, the one named last changes fastest.
Arguments:
- feats: bfloat16 [32, 128, 384], P('seq', None, 'grp'), may hold values from -6 to 6
- conv_weight: bfloat16 [3, 128, 128], replicated, may hold values from -0.3125 to 0.3125
- conv_bias: float32 [128], replicated, may hold values from -3 to 3
- latent_projection_weight: bfloat16 [16, 128], replicated, may hold values from -0.75 to 0.75
- noise: bfloat16 [32, 16, 384], P('seq', None, 'grp'), may hold values from -6 to 6
- step_index: int32 [1], replicated, may hold values from 0 to 49
- hist: bfloat16 [128, 64], P('seq'), may hold values from -6 to 6
- hist_level: int32 [128], P('seq'), may hold values from 0 to 2
- hist_count: int32 [16], replicated, may hold values from 1 to 8, 96 in all
- w_in: bfloat16 [64, 3072], replicated, may hold values from -2 to 2
- w_hist: bfloat16 [3, 64, 3072], replicated, may hold values from -0.75 to 0.75
- norm_gain: float32 [3072], replicated, may hold values from 0.5 to 2
- w_query: bfloat16 [3072, 1536], P(None, 'grp'), may hold values from -2 to 2
- w_key: bfloat16 [3072, 1536], P(None, 'grp'), may hold values from -2 to 2
- w_value: bfloat16 [3072, 1536], P(None, 'grp'), may hold values from -0.109375 to 0.109375
- q_gain: float32 [128], replicated, may hold values from 0.5 to 6
- k_gain: float32 [128], replicated, may hold values from 0.5 to 6
- w_out: bfloat16 [1536, 3072], P('grp'), may hold values from -0.5 to 0.5
Outputs:
- attention_out: bfloat16 [3072, 3072], P('seq', 'grp')
Inputs may be any that keep to these rules, and one draw needn't show every extreme that they name: hist_count[s] of the 8 history slots of seq index s are live; the largest count is exactly 8.
All inputs are finite; a program needn't handle non-finite values.
Results may differ from a plain program's by a relative error of at most 0.0095.
The roundings to bfloat16 on the way count: a program that leaves them out, or rounds other values in their place, can miss the bound.
Values may be sent and summed in bfloat16 or wider, within the bound.
No kernel may reach another device: no remote copies, remote signals or barrier semaphores. Data moves between devices by JAX's collectives and lax.ppermute only.
A program may use at most 256 MiB of HBM per device.

v0:
```python
import math
import jax
import jax.numpy as jnp
from jax import lax
from jax.sharding import PartitionSpec as P

STEPS = 50
EPSILON = 1e-06


def from_behind(value, axis, steps):
    count = lax.axis_size(axis)
    initial, last = (max(0, -steps), min(count, count - steps))
    return lax.ppermute(value, axis, [(source, source + steps) for source in range(initial, last)])


def time_embed(step_index, width):
    half_width = width // 2
    frequency = jnp.exp(-math.log(10000.0) * jnp.arange(half_width, dtype=jnp.float32) / half_width)
    angles = step_index[0].astype(jnp.float32) * frequency
    return jnp.concatenate([jnp.cos(angles), jnp.sin(angles)])


def rms_scale(values, gain):
    return values * lax.rsqrt(jnp.mean(values * values, axis=-1, keepdims=True) + EPSILON) * gain


def local(
    feats,
    conv_weight,
    conv_bias,
    latent_projection_weight,
    noise,
    step_index,
    hist,
    hist_level,
    hist_count,
    w_in,
    w_hist,
    norm_gain,
    w_query,
    w_key,
    w_value,
    q_gain,
    k_gain,
    w_out,
):
    frame_count, channels, pixels = feats.shape
    earlier = from_behind(feats, "seq", 1)
    padded = jnp.concatenate([earlier, feats], axis=0)
    total = jnp.zeros(feats.shape, jnp.float32)
    for tap_index in range(3):
        window = padded[2 - tap_index : 2 - tap_index + frame_count]
        total = total + jnp.einsum(
            "oc,tcp->top", conv_weight[tap_index], window, preferred_element_type=jnp.float32
        )
    hidden_state = jax.nn.silu(total + conv_bias[None, :, None]).astype(jnp.bfloat16)
    sigma = (STEPS - step_index[0].astype(jnp.float32)) / STEPS
    latent_input = jnp.einsum(
        "qb,zby->zqy", latent_projection_weight, hidden_state, preferred_element_type=jnp.float32
    )
    noisy = ((1.0 - sigma) * latent_input + sigma * noise.astype(jnp.float32)).astype(jnp.bfloat16)
    lat_channels = noisy.shape[1]
    patches = (
        noisy.reshape(frame_count, lat_channels, pixels // 4, 4)
        .transpose(0, 2, 1, 3)
        .reshape(frame_count, pixels // 4, lat_channels * 4)
    )
    width = w_in.shape[1]
    embed = time_embed(step_index, width)
    all_patches = lax.all_gather(patches, "grp", axis=1, tiled=True)
    block_rows = all_patches.shape[1]
    summed = (
        jnp.dot(
            all_patches.reshape(-1, all_patches.shape[2]), w_in, preferred_element_type=jnp.float32
        )
        + embed
    )
    tokens = (
        rms_scale(summed, norm_gain)
        .astype(jnp.bfloat16)
        .reshape(frame_count, block_rows, width)
        .reshape(-1, width)
    )
    history = jnp.zeros((hist.shape[0], width), jnp.float32)
    for level in range(3):
        history = (
            history
            + jnp.dot(hist, w_hist[level], preferred_element_type=jnp.float32)
            * (hist_level == level).astype(jnp.float32)[:, None]
        )
    history = rms_scale(history, norm_gain).astype(jnp.bfloat16)
    both_rows = jnp.concatenate([tokens, history], axis=0)
    sec_rows = tokens.shape[0]
    key_rows = both_rows.shape[0]
    head_size = q_gain.shape[0]
    heads_local = w_query.shape[1] // head_size
    query = rms_scale(
        jnp.dot(tokens, w_query, preferred_element_type=jnp.float32).reshape(
            sec_rows, heads_local, head_size
        ),
        q_gain,
    ).astype(jnp.bfloat16)
    flattened_keys = (
        rms_scale(
            jnp.dot(both_rows, w_key, preferred_element_type=jnp.float32).reshape(
                key_rows, heads_local, head_size
            ),
            k_gain,
        )
        .astype(jnp.bfloat16)
        .reshape(key_rows, heads_local * head_size)
    )
    values_flat = jnp.dot(both_rows, w_value, preferred_element_type=jnp.float32).astype(
        jnp.bfloat16
    )
    seq_count = lax.axis_size("seq")
    shard_ids = jnp.arange(seq_count, dtype=jnp.int32)
    scale = 1.0 / math.sqrt(head_size)
    run_max = jnp.full((heads_local, sec_rows), -1e30, jnp.float32)
    key_piece = lax.all_gather(flattened_keys, "seq", axis=0, tiled=True)
    value_piece = lax.all_gather(values_flat, "seq", axis=0, tiled=True)
    count_rows = key_piece.shape[0]
    row_index = jnp.arange(count_rows, dtype=jnp.int32)
    owner = row_index // key_rows
    local_index = row_index - owner * key_rows
    owner_count = jnp.sum(
        jnp.where(owner[:, None] == shard_ids[None, :], hist_count[None, :], 0), axis=1
    )
    alive = (local_index < sec_rows) | (local_index - sec_rows < owner_count)
    key_heads = key_piece.reshape(count_rows, heads_local, head_size)
    value_heads = value_piece.reshape(count_rows, heads_local, head_size)
    scores = (
        jnp.einsum("qhd,khd->hqk", query, key_heads, preferred_element_type=jnp.float32) * scale
    )
    scores = jnp.where(alive[None, None, :], scores, -1e30)
    new_max = jnp.maximum(run_max, jnp.max(scores, axis=-1))
    soft = jnp.where(alive[None, None, :], jnp.exp(scores - new_max[..., None]), 0.0)
    new_sum = jnp.sum(soft, axis=-1)
    new_weighted = jnp.einsum(
        "hqk,khd->hqd", soft.astype(jnp.bfloat16), value_heads, preferred_element_type=jnp.float32
    )
    attended = new_weighted / new_sum[..., None]
    heads_out = (
        attended.astype(jnp.bfloat16).transpose(1, 0, 2).reshape(sec_rows, heads_local * head_size)
    )
    partial_out = jnp.dot(heads_out, w_out, preferred_element_type=jnp.float32)
    return lax.psum_scatter(
        partial_out.astype(jnp.bfloat16), "grp", scatter_dimension=1, tiled=True
    )


def solution(mesh):
    placed = (
        P("seq", None, "grp"),
        P(),
        P(),
        P(),
        P("seq", None, "grp"),
        P(),
        P("seq", None),
        P("seq"),
        P(),
        P(),
        P(),
        P(),
        P(None, "grp"),
        P(None, "grp"),
        P(None, "grp"),
        P(),
        P(),
        P("grp", None),
    )
    return jax.shard_map(
        local, mesh=mesh, in_specs=placed, out_specs=P("seq", "grp"), check_vma=False
    )
```

profile of v0, /device:TPU:0, one launch (start us, length us, event | category | flops | bytes accessed | tf_op | source)
XLA Modules:
  0.0 191.2 jit_solution(1770931649743177877)
XLA Ops:
  6.5 2.5 %collective-permute-start = (bf16[2,128,192]{1,2,0:T(8,128)(2,1)}, bf16[2,128,192]{1,2,0:T(8,128)(2,1)S(1)}, u32[]{:S(2)}, u32[]{:S(2)}) collective-permute-start(bf16[2,128,192]{1,2,0:T(8,128)(2,1)} %param.18), channel_id=1, source_target_pairs={{0,1},{1,2},{2,3},{3,4},{4,5},{5,6},{6,7},{7,8},{8,9},{9,10},{10,1... | collective-permute-start | bytes 294920 | tf_op jit(solution)/shard_map/ppermute | solution.py:14
  9.8 1.1 fusion.46
  11.5 1.2 convolution_multiply_fusion.2
  12.7 1.2 fusion.7
  13.9 1.3 multiply_reduce_fusion.2
  15.9 0.8 multiply_convert_fusion.3
  16.7 1.0 convolution_add_fusion.2
  17.7 1.1 fusion.15
  19.1 4.8 %all_gather.9 = bf16[2,96,64]{2,0,1:T(2,128)(2,1)S(1)} all-gather(bf16[2,48,64]{2,0,1:T(2,128)(2,1)S(1)} %copy.73), channel_id=1, replica_groups=mesh['grp'=2,'seq'=16] {'grp'}, dimensions={1}, use_global_device_ids=true | all-gather | bytes 36864 | tf_op jit(solution)/shard_map/all_gather | solution.py:71
  25.1 1.4 copy-done.5
  26.5 2.0 %fusion.66 = (f32[200,768]{1,0:T(8,128)}, f32[200,768]{1,0:T(8,128)S(1)}) fusion(bf16[3072,768]{1,0:T(8,128)(2,1)S(1)} %copy-done.5, bf16[8,3072]{1,0:T(8,128)(2,1)S(1)} %multiply_convert_fusion.3, bf16[192,3072]{1,0:T(8,128)(2,1)S(1)} %multiply_convert_fusion), kind=kOutput, calls=%fused_computation.94 | convolution fusion | flops 946329600 | bytes 7176192 | tf_op jit(solution)/shard_map/dot_general | solution.py:106
  28.5 1.2 mul.185
  30.5 0.9 fusion.27
  31.4 4.2 %convolution_convert_fusion.1 = bf16[200,768]{1,0:T(8,128)(2,1)} fusion(bf16[3072,768]{1,0:T(8,128)(2,1)} %param.32, bf16[8,3072]{1,0:T(8,128)(2,1)S(1)} %multiply_convert_fusion.3, bf16[192,3072]{1,0:T(8,128)(2,1)S(1)} %multiply_convert_fusion), kind=kOutput, calls=%fused_computation.18 | convolution fusion | flops 946329600 | bytes 6254592 | tf_op jit(solution)/shard_map/dot_general | solution.py:114
  35.9 3.4 %fusion.67 = f32[192,768]{1,0:T(8,128)S(1)} fusion(bf16[192,3072]{1,0:T(8,128)(2,1)S(1)} %multiply_convert_fusion, bf16[3072,768]{1,0:T(8,128)(2,1)} %param.30), kind=kOutput, calls=%fused_computation.95 | convolution fusion | flops 905969664 | bytes 6488064 | tf_op jit(solution)/shard_map/dot_general | solution.py:99
  40.2 47.4 %all-gather.3.cloned.1.call-done = bf16[3200,768]{1,0:T(8,128)(2,1)} async-done(((bf16[200,768]{1,0:T(8,128)(2,1)}), bf16[3200,768]{1,0:T(8,128)(2,1)}) %all-gather.3.cloned.1.call-update) | async-done | bytes 4915216 | tf_op jit(solution)/shard_map/all_gather | solution.py:121
  87.6 7.4 %copy.79 = bf16[3200,768]{0,1:T(8,128)(2,1)} copy(bf16[3200,768]{1,0:T(8,128)(2,1)} %all-gather.3.cloned.1.call-done) | data formatting | bytes 9830400 | tf_op jit(solution)/shard_map/all_gather | solution.py:121
  95.1 10.4 %fusion = (f32[6,192]{1,0:T(8,128)S(1)}, f32[6,192,3200]{2,1,0:T(8,128)}) fusion(pred[3200]{0:T(1024)(128)(4,1)S(1)} %fusion.54, bf16[3200,6,128]{0,2,1:T(8,128)(2,1)} %bitcast.85, bf16[192,6,128]{2,1,0:T(8,128)(2,1)S(1)} %multiply_convert_fusion.1), kind=kOutput, calls=%fused_computation.2 | convolution fusion | flops 954776448 | bytes 19963520 | tf_op jit(solution)/shard_map/qhd,khd->hqk/dot_general | solution.py:134
  105.4 9.1 %fusion.1 = f32[6,192]{1,0:T(8,128)S(1)} fusion(f32[6,192,3200]{2,1,0:T(8,128)} %get-tuple-element.15, f32[6,192]{1,0:T(8,128)S(1)} %broadcast_maximum_fusion, pred[3200]{0:T(1024)(128)(4,1)S(1)} %fusion.54), kind=kLoop, calls=%fused_computation.3 | loop fusion | flops 18430848 | bytes 14758016 | tf_op jit(solution)/shard_map/reduce_sum | solution.py:139
  114.5 28.0 %all-gather.5.cloned.1.call-done = bf16[3200,768]{1,0:T(8,128)(2,1)} async-done(((bf16[200,768]{1,0:T(8,128)(2,1)}), bf16[3200,768]{1,0:T(8,128)(2,1)}) %all-gather.5.cloned.1.call-update) | async-done | bytes 4915216 | tf_op jit(solution)/shard_map/all_gather | solution.py:122
  142.5 7.4 %copy.82 = bf16[3200,768]{0,1:T(8,128)(2,1)} copy(bf16[3200,768]{1,0:T(8,128)(2,1)} %all-gather.5.cloned.1.call-done) | data formatting | bytes 9830400 | tf_op jit(solution)/shard_map/all_gather | solution.py:122
  149.9 9.7 %fusion.22 = bf16[6,24,8,128]{3,2,1,0:T(8,128)(2,1)S(1)} fusion(bf16[3200,6,128]{0,2,1:T(8,128)(2,1)} %bitcast.86, f32[6,192,3200]{2,1,0:T(8,128)} %get-tuple-element.15, f32[6,192]{1,0:T(8,128)S(1)} %broadcast_maximum_fusion, pred[3200]{0:T(1024)(128)(4,1)S(1)} %fusion.54, f32[192,6]{0,1:T(8,128)S(1)} %bitcast.90), kind=kOutput, calls=%fused_computation.29 | convolution fusion | flops 962445312 | bytes 19968128 | tf_op jit(solution)/shard_map/hqk,khd->hqd/dot_general | solution.py:140
  159.6 4.4 %convolution_convert_fusion = bf16[192,3072]{1,0:T(8,128)(2,1)} fusion(bf16[768,3072]{1,0:T(8,128)(2,1)} %param.35, bf16[6,24,8,128]{3,2,1,0:T(8,128)(2,1)S(1)} %fusion.22), kind=kOutput, calls=%fused_computation.8 | convolution fusion | flops 906559488 | bytes 6193152 | tf_op jit(solution)/shard_map/dot_general | solution.py:147
  164.1 20.5 %reduce-scatter.2.cloned.1.call-done = bf16[192,1536]{1,0:T(8,128)(2,1)} async-done(((bf16[192,3072]{1,0:T(8,128)(2,1)}), bf16[192,1536]{1,0:T(8,128)(2,1)}) %reduce-scatter.2.cloned.1.call-update) | async-done | bytes 589840 | tf_op jit(solution)/shard_map/reduce_scatter | solution.py:148
  (46 shorter events, 4.8 us)
Async XLA Ops:
  6.5 17.6 %copy-start = (bf16[64,3072]{1,0:T(8,128)(2,1)S(1)}, bf16[64,3072]{1,0:T(8,128)(2,1)}, u32[]{:S(2)}) copy-start(bf16[64,3072]{1,0:T(8,128)(2,1)} %param.27) | copy-start | bytes 1179652
  6.5 18.2 %copy-start.2 = (f32[3072]{0:T(1024)S(1)}, f32[3072]{0:T(1024)}, u32[]{:S(2)}) copy-start(f32[3072]{0:T(1024)} %param.29) | copy-start | bytes 36868
  6.5 81.1 %all-gather.3.cloned.1.call-start = ((), (), s32[]{:S(2)}) async-start(), calls=%async_computation.1 | async-start | bytes 5222400 | tf_op jit(solution)/shard_map/all_gather | solution.py:121
  6.5 10.1 %collective-permute-start = (bf16[2,128,192]{1,2,0:T(8,128)(2,1)}, bf16[2,128,192]{1,2,0:T(8,128)(2,1)S(1)}, u32[]{:S(2)}, u32[]{:S(2)}) collective-permute-start(bf16[2,128,192]{1,2,0:T(8,128)(2,1)} %param.18), channel_id=1, source_target_pairs={{0,1},{1,2},{2,3},{3,4},{4,5},{5,6},{6,7},{7,8},{8,9},{9,10},{10,1... | collective-permute-start | bytes 294920 | tf_op jit(solution)/shard_map/ppermute | solution.py:14
  24.1 2.3 %copy-start.5 = (bf16[3072,768]{1,0:T(8,128)(2,1)S(1)}, bf16[3072,768]{1,0:T(8,128)(2,1)}, u32[]{:S(2)}) copy-start(bf16[3072,768]{1,0:T(8,128)(2,1)} %param.31) | copy-start | bytes 14155780
  30.5 5.3 %copy-start.3 = (s32[16]{0:T(128)S(1)}, s32[16]{0:T(128)}, u32[]{:S(2)}) copy-start(s32[16]{0:T(128)} %param.26) | copy-start | bytes 196
  31.4 111.1 %all-gather.5.cloned.1.call-start = ((), (), s32[]{:S(2)}) async-start(), calls=%async_computation.2 | async-start | bytes 5222400 | tf_op jit(solution)/shard_map/all_gather | solution.py:122
  35.6 4.3 %copy-start.4 = (f32[128]{0:T(128)S(1)}, f32[128]{0:T(128)}, u32[]{:S(2)}) copy-start(f32[128]{0:T(128)} %param.33) | copy-start | bytes 1540
  35.7 149.0 %reduce-scatter.2.cloned.1.call-start = ((), (), s32[]{:S(2)}) async-start(), calls=%async_computation.3 | async-start | bytes 1769472 | tf_op jit(solution)/shard_map/reduce_scatter | solution.py:148
  149.9 34.7 %copy-start.1 = (bf16[64,3072]{1,0:T(8,128)(2,1)S(1)}, bf16[64,3072]{1,0:T(8,128)(2,1)}, u32[]{:S(2)}) copy-start(bf16[64,3072]{1,0:T(8,128)(2,1)} %param.27) | copy-start | bytes 1179652
Sparse Core Ops, SparseCore 0:
  31.5 56.0 all-gather.2
  89.8 52.6 all-gather.4
  164.2 20.3 reduce-scatter.1
where the time goes:
time: 192 us; the launch traced here: 191 us
  waiting for transfers between devices  96 us (50%)
  matrix products  41.5 us (22%)
  local copies, waits for them, and re-layouts  19.5 us (10%)
  between operations  14 us (7%)
  other arithmetic  12.8 us (7%)
  blocking collectives  4.77 us (2%)
  starting transfers between devices  2.61 us (1%)
    all_gather x1, waiting for transfers between devices, local(): key_piece = lax.all_gather(flattened_keys, 'seq', axis=0, tiled=True)  47.4 us
    all_gather x1, waiting for transfers between devices, local(): value_piece = lax.all_gather(values_flat, 'seq', axis=0, tiled=True)  28 us
    reduce_scatter x1, waiting for transfers between devices, local(): lax.psum_scatter(partial_out.astype(jnp.bfloat16), 'grp', scatter_dimensi...  20.5 us
    dot_general x1, matrix products, local(): jnp.einsum('qhd,khd->hqk', query, key_heads, preferred_element_type=jnp.f...  10.4 us
    dot_general x1, matrix products, local(): jnp.einsum('hqk,khd->hqd', soft.astype(jnp.bfloat16), value_heads, prefer...  9.68 us
    reduce_sum x1, other arithmetic, local(): new_sum = jnp.sum(soft, axis=-1)  9.09 us
    all_gather x1, local copies, waits for them, and re-layouts, local(): key_piece = lax.all_gather(flattened_keys, 'seq', axis=0, tiled=True)  7.44 us
    all_gather x1, local copies, waits for them, and re-layouts, local(): value_piece = lax.all_gather(values_flat, 'seq', axis=0, tiled=True)  7.44 us
  transfers between devices with their start and end apart: 4, of which 3 were waited for; matrix products, arithmetic and copies ran while one was open for 22% of the time, Pallas kernels for 0%

commit v1 on v0

--- a/solution.py
+++ b/solution.py
@@ -6,6 +6,12 @@
 
 STEPS = 50
 EPSILON = 1e-06
+
+
+def in_order(tiles, dim):
+    tiles = jnp.moveaxis(tiles, 0, dim)
+    shape = tiles.shape
+    return tiles.reshape(*shape[:dim], shape[dim] * shape[dim + 1], *shape[dim + 2 :])
 
 
 def from_behind(value, axis, steps):
@@ -119,7 +125,19 @@
     scale = 1.0 / math.sqrt(head_size)
     run_max = jnp.full((heads_local, sec_rows), -1e30, jnp.float32)
     key_piece = lax.all_gather(flattened_keys, "seq", axis=0, tiled=True)
-    value_piece = lax.all_gather(values_flat, "seq", axis=0, tiled=True)
+    size = lax.axis_size("seq")
+    pairs = [(i, (i + 1) % size) for i in range(size)]
+    back = [(b, a) for a, b in pairs]
+    lower, upper = ([], [])
+    for lap in range(size - 1):
+        if lap % 2 == 0:
+            lower.append(lax.ppermute(lower[-1] if lower else values_flat, "seq", pairs))
+        else:
+            upper.append(lax.ppermute(upper[-1] if upper else values_flat, "seq", back))
+    parts = jnp.stack([*lower[::-1], values_flat, *upper])
+    shift = lax.axis_index("seq") - len(lower)
+    parts = parts[(jnp.arange(size) - shift) % size]
+    value_piece = in_order(parts, 0)
     count_rows = key_piece.shape[0]
     row_index = jnp.arange(count_rows, dtype=jnp.int32)
     owner = row_index // key_rows

time: 192 us -> 227 us (1.18)
  starting transfers between devices: 2.61 us -> 35.9 us
  local copies, waits for them, and re-layouts: 19.5 us -> 49.4 us
  waiting for transfers between devices: 96 us -> 68.6 us
    ppermute x0 -> x15, waiting for transfers between devices: none -> 49.3 us  [the longest x8 37.2 us: local(): lax.ppermute(lower[-1] if lower else values_flat, 'seq', pairs)]
    all_gather x1, waiting for transfers between devices: 47.4 us -> 0.01 us  [local(): key_piece = lax.all_gather(flattened_keys, 'seq', axis=0, tiled=True)]
    ppermute x0 -> x15, starting transfers between devices: none -> 33.4 us  [the longest x7 32 us: local(): upper.append(lax.ppermute(upper[-1] if upper else values_flat, 'seq', back))]
    all_gather x1 -> x0, waiting for transfers between devices: 28 us -> none  [local(): value_piece = lax.all_gather(values_flat, 'seq', axis=0, tiled=True)]
    unnamed x12 -> x43, local copies, waits for them, and re-layouts: 1.41 us -> 21.3 us
    another operation x0 -> x2, local copies, waits for them, and re-layouts: none -> 12 us  [the longest x1 11.2 us: local(): value_heads = value_piece.reshape(count_rows, heads_local, head_size)]
    all_gather x1 -> x0, local copies, waits for them, and re-layouts: 7.44 us -> none  [local(): value_piece = lax.all_gather(values_flat, 'seq', axis=0, tiled=True)]
    gather x0 -> x1, local copies, waits for them, and re-layouts: none -> 5.55 us  [local(): parts = parts[(jnp.arange(size) - shift) % size]]
  transfers between devices with their start and end apart: 4 -> 18, of which waited for: 3 -> 13; matrix products, arithmetic and copies ran while one was open for 22% -> 23% of each run, Pallas kernels for 0% -> 0%
where the time goes in v1:
time: 227 us; the launch traced here: 226 us
  waiting for transfers between devices  68.6 us (30%)
  local copies, waits for them, and re-layouts  49.4 us (22%)
  matrix products  40 us (18%)
  starting transfers between devices  35.9 us (16%)
  between operations  14.4 us (6%)
  other arithmetic  13 us (6%)
  blocking collectives  4.76 us (2%)
    ppermute x8, waiting for transfers between devices, local(): lax.ppermute(lower[-1] if lower else values_flat, 'seq', pairs)  37.2 us
    ppermute x7, starting transfers between devices, local(): upper.append(lax.ppermute(upper[-1] if upper else values_flat, 'seq', back))  32 us
    unnamed x43, local copies, waits for them, and re-layouts  21.3 us
    reduce_scatter x1, waiting for transfers between devices, local(): lax.psum_scatter(partial_out.astype(jnp.bfloat16), 'grp', scatter_dimensi...  19.3 us
    ppermute x7, waiting for transfers between devices, local(): upper.append(lax.ppermute(upper[-1] if upper else values_flat, 'seq', back))  12 us
    dot_general x1, matrix products, local(): jnp.einsum('hqk,khd->hqd', soft.astype(jnp.bfloat16), value_heads, prefer...  11.3 us
    another operation x1, local copies, waits for them, and re-layouts, local(): value_heads = value_piece.reshape(count_rows, heads_local, head_size)  11.2 us
    dot_general x1, matrix products, local(): jnp.einsum('qhd,khd->hqk', query, key_heads, preferred_element_type=jnp.f...  10.2 us
  transfers between devices with their start and end apart: 18, of which 13 were waited for; matrix products, arithmetic and copies ran while one was open for 23% of the time, Pallas kernels for 0%

profile of v1, /device:TPU:0, one launch (start us, length us, event | category | flops | bytes accessed | tf_op | source)
XLA Modules:
  0.0 226.0 jit_solution(6816570353035609079)
XLA Ops:
  19.2 4.8 %all_gather.6 = bf16[2,96,64]{2,0,1:T(2,128)(2,1)S(1)} all-gather(bf16[2,48,64]{2,0,1:T(2,128)(2,1)S(1)} %copy.73), channel_id=1, replica_groups=mesh['grp'=2,'seq'=16] {'grp'}, dimensions={1}, use_global_device_ids=true | all-gather | bytes 36864 | tf_op jit(solution)/shard_map/all_gather | solution.py:77
  31.4 3.5 %convolution_convert_fusion.1 = bf16[200,768]{1,0:T(8,128)(2,1)S(1)} fusion(bf16[3072,768]{1,0:T(8,128)(2,1)} %param.32, bf16[8,3072]{1,0:T(8,128)(2,1)S(1)} %multiply_convert_fusion.3, bf16[192,3072]{1,0:T(8,128)(2,1)S(1)} %multiply_convert_fusion), kind=kOutput, calls=%fused_computation.20 | convolution fusion | flops 946329600 | bytes 6254592 | tf_op jit(solution)/shard_map/dot_general | solution.py:120
  36.2 7.8 %collective-permute-done.1 = bf16[200,768]{1,0:T(8,128)(2,1)S(1)} collective-permute-done((bf16[200,768]{1,0:T(8,128)(2,1)S(1)}, bf16[200,768]{1,0:T(8,128)(2,1)S(1)}, u32[]{:S(2)}, u32[]{:S(2)}) %collective-permute-start.1) | collective-permute-done | bytes 307232 | tf_op jit(solution)/shard_map/ppermute | solution.py:134
  44.0 4.4 %collective-permute-start.9 = (bf16[200,768]{1,0:T(8,128)(2,1)S(1)}, bf16[200,768]{1,0:T(8,128)(2,1)S(1)}, u32[]{:S(2)}, u32[]{:S(2)}) collective-permute-start(bf16[200,768]{1,0:T(8,128)(2,1)S(1)} %convolution_convert_fusion.1), channel_id=1, source_target_pairs={{1,0},{2,1},{3,2},{4,3},{5,4},{6,5},{7,6},{8,7},{9,8},{10,9},{11,1... | collective-permute-start | bytes 921608 | tf_op jit(solution)/shard_map/ppermute | solution.py:136
  48.4 11.2 %collective-permute-done.2 = bf16[200,768]{1,0:T(8,128)(2,1)S(1)} collective-permute-done((bf16[200,768]{1,0:T(8,128)(2,1)S(1)}, bf16[200,768]{1,0:T(8,128)(2,1)S(1)}, u32[]{:S(2)}, u32[]{:S(2)}) %collective-permute-start.2) | collective-permute-done | bytes 307232 | tf_op jit(solution)/shard_map/ppermute | solution.py:134
  59.7 4.4 %collective-permute-start.10 = (bf16[200,768]{1,0:T(8,128)(2,1)S(1)}, bf16[200,768]{1,0:T(8,128)(2,1)S(1)}, u32[]{:S(2)}, u32[]{:S(2)}) collective-permute-start(bf16[200,768]{1,0:T(8,128)(2,1)S(1)} %collective-permute-done.9), channel_id=1, source_target_pairs={{1,0},{2,1},{3,2},{4,3},{5,4},{6,5},{7,6},{8,7},{9,8},{10,9},{11,1... | collective-permute-start | bytes 921608 | tf_op jit(solution)/shard_map/ppermute | solution.py:136
  64.1 5.7 %collective-permute-done.3 = bf16[200,768]{1,0:T(8,128)(2,1)S(1)} collective-permute-done((bf16[200,768]{1,0:T(8,128)(2,1)S(1)}, bf16[200,768]{1,0:T(8,128)(2,1)S(1)}, u32[]{:S(2)}, u32[]{:S(2)}) %collective-permute-start.3) | collective-permute-done | bytes 307232 | tf_op jit(solution)/shard_map/ppermute | solution.py:134
  69.8 5.1 %collective-permute-done.10 = bf16[200,768]{1,0:T(8,128)(2,1)S(1)} collective-permute-done((bf16[200,768]{1,0:T(8,128)(2,1)S(1)}, bf16[200,768]{1,0:T(8,128)(2,1)S(1)}, u32[]{:S(2)}, u32[]{:S(2)}) %collective-permute-start.10) | collective-permute-done | bytes 307232 | tf_op jit(solution)/shard_map/ppermute | solution.py:136
  74.9 4.6 %collective-permute-start.11 = (bf16[200,768]{1,0:T(8,128)(2,1)S(1)}, bf16[200,768]{1,0:T(8,128)(2,1)S(1)}, u32[]{:S(2)}, u32[]{:S(2)}) collective-permute-start(bf16[200,768]{1,0:T(8,128)(2,1)S(1)} %collective-permute-done.10), channel_id=1, source_target_pairs={{1,0},{2,1},{3,2},{4,3},{5,4},{6,5},{7,6},{8,7},{9,8},{10,9},{11,1... | collective-permute-start | bytes 921608 | tf_op jit(solution)/shard_map/ppermute | solution.py:136
  79.5 3.9 %collective-permute-done.4 = bf16[200,768]{1,0:T(8,128)(2,1)} collective-permute-done((bf16[200,768]{1,0:T(8,128)(2,1)S(1)}, bf16[200,768]{1,0:T(8,128)(2,1)}, u32[]{:S(2)}, u32[]{:S(2)}) %collective-permute-start.4) | collective-permute-done | bytes 307232 | tf_op jit(solution)/shard_map/ppermute | solution.py:134
  85.5 4.6 %collective-permute-start.12 = (bf16[200,768]{1,0:T(8,128)(2,1)S(1)}, bf16[200,768]{1,0:T(8,128)(2,1)}, u32[]{:S(2)}, u32[]{:S(2)}) collective-permute-start(bf16[200,768]{1,0:T(8,128)(2,1)S(1)} %collective-permute-done.11), channel_id=1, source_target_pairs={{1,0},{2,1},{3,2},{4,3},{5,4},{6,5},{7,6},{8,7},{9,8},{10,9},{11,1... | collective-permute-start | bytes 921608 | tf_op jit(solution)/shard_map/ppermute | solution.py:136
  94.5 4.9 %collective-permute-start.13 = (bf16[200,768]{1,0:T(8,128)(2,1)}, bf16[200,768]{1,0:T(8,128)(2,1)}, u32[]{:S(2)}, u32[]{:S(2)}) collective-permute-start(bf16[200,768]{1,0:T(8,128)(2,1)} %collective-permute-done.12), channel_id=1, source_target_pairs={{1,0},{2,1},{3,2},{4,3},{5,4},{6,5},{7,6},{8,7},{9,8},{10,9},{11,1... | collective-permute-start | bytes 921608 | tf_op jit(solution)/shard_map/ppermute | solution.py:136
  99.4 3.9 %collective-permute-done.6 = bf16[200,768]{1,0:T(8,128)(2,1)} collective-permute-done((bf16[200,768]{1,0:T(8,128)(2,1)S(1)}, bf16[200,768]{1,0:T(8,128)(2,1)}, u32[]{:S(2)}, u32[]{:S(2)}) %collective-permute-start.6) | collective-permute-done | bytes 307232 | tf_op jit(solution)/shard_map/ppermute | solution.py:134
  103.4 3.4 %fusion.78 = f32[192,768]{1,0:T(8,128)S(1)} fusion(bf16[192,3072]{1,0:T(8,128)(2,1)S(1)} %multiply_convert_fusion, bf16[3072,768]{1,0:T(8,128)(2,1)} %param.30), kind=kOutput, calls=%fused_computation.120 | convolution fusion | flops 905969664 | bytes 6488064 | tf_op jit(solution)/shard_map/dot_general | solution.py:105
  107.3 4.4 %collective-permute-start.14 = (bf16[200,768]{1,0:T(8,128)(2,1)}, bf16[200,768]{1,0:T(8,128)(2,1)}, u32[]{:S(2)}, u32[]{:S(2)}) collective-permute-start(bf16[200,768]{1,0:T(8,128)(2,1)} %collective-permute-done.13), channel_id=1, source_target_pairs={{1,0},{2,1},{3,2},{4,3},{5,4},{6,5},{7,6},{8,7},{9,8},{10,9},{11,1... | collective-permute-start | bytes 921608 | tf_op jit(solution)/shard_map/ppermute | solution.py:136
  113.2 3.2 %collective-permute-done.14 = bf16[200,768]{1,0:T(8,128)(2,1)} collective-permute-done((bf16[200,768]{1,0:T(8,128)(2,1)}, bf16[200,768]{1,0:T(8,128)(2,1)}, u32[]{:S(2)}, u32[]{:S(2)}) %collective-permute-start.14) | collective-permute-done | bytes 307232 | tf_op jit(solution)/shard_map/ppermute | solution.py:136
  116.4 4.6 %collective-permute-start.15 = (bf16[200,768]{1,0:T(8,128)(2,1)}, bf16[200,768]{1,0:T(8,128)(2,1)S(1)}, u32[]{:S(2)}, u32[]{:S(2)}) collective-permute-start(bf16[200,768]{1,0:T(8,128)(2,1)} %collective-permute-done.14), channel_id=1, source_target_pairs={{1,0},{2,1},{3,2},{4,3},{5,4},{6,5},{7,6},{8,7},{9,8},{10,9},{11,1... | collective-permute-start | bytes 921608 | tf_op jit(solution)/shard_map/ppermute | solution.py:136
  142.8 5.6 %gather_fusion = bf16[16,200,768]{2,1,0:T(8,128)(2,1)} fusion(bf16[16,200,768]{2,1,0:T(8,128)(2,1)} %bitcast_dynamic-update-slice_fusion, s32[1024]{0:T(1024)S(1)} %pad_clamp_fusion), kind=kCustom, calls=%fused_computation | custom fusion | bytes 9830464 | tf_op jit(solution)/shard_map/gather | solution.py:139
  148.3 11.2 %reshape.171 = bf16[3200,6,128]{2,1,0:T(8,128)(2,1)} reshape(bf16[16,200,768]{2,1,0:T(8,128)(2,1)} %gather_fusion) | data formatting | bytes 9830400 | tf_op jit(solution)/shard_map/reshape;reshape | solution.py:150
  159.5 7.4 %copy.79 = bf16[3200,768]{0,1:T(8,128)(2,1)} copy(bf16[3200,768]{1,0:T(8,128)(2,1)} %all-gather.2.cloned.1.call-done) | data formatting | bytes 9830400 | tf_op jit(solution)/shard_map/all_gather | solution.py:127
  167.0 10.2 %fusion = (f32[6,192]{1,0:T(8,128)S(1)}, f32[6,192,3200]{2,1,0:T(8,128)}) fusion(pred[3200]{0:T(1024)(128)(4,1)S(1)} %fusion.63, bf16[3200,6,128]{0,2,1:T(8,128)(2,1)} %bitcast.117, bf16[192,6,128]{2,1,0:T(8,128)(2,1)S(1)} %multiply_convert_fusion.1), kind=kOutput, calls=%fused_computation.3 | convolution fusion | flops 954776448 | bytes 19963520 | tf_op jit(solution)/shard_map/qhd,khd->hqk/dot_general | solution.py:152
  177.1 9.2 %fusion.1 = f32[6,192]{1,0:T(8,128)S(1)} fusion(f32[6,192,3200]{2,1,0:T(8,128)} %get-tuple-element.15, f32[6,192]{1,0:T(8,128)S(1)} %broadcast_maximum_fusion, pred[3200]{0:T(1024)(128)(4,1)S(1)} %fusion.63), kind=kLoop, calls=%fused_computation.4 | loop fusion | flops 18430848 | bytes 14758016 | tf_op jit(solution)/shard_map/reduce_sum | solution.py:157
  186.3 11.3 %fusion.29 = bf16[6,24,8,128]{3,2,1,0:T(8,128)(2,1)S(1)} fusion(bf16[3200,6,128]{2,1,0:T(8,128)(2,1)} %reshape.171, f32[6,192,3200]{2,1,0:T(8,128)} %get-tuple-element.15, f32[6,192]{1,0:T(8,128)S(1)} %broadcast_maximum_fusion, pred[3200]{0:T(1024)(128)(4,1)S(1)} %fusion.63, f32[192,6]{0,1:T(8,128)S(1)} %bitcast.123), kind=kOutput, calls=%fused_computation.31 | convolution fusion | flops 962445312 | bytes 19968128 | tf_op jit(solution)/shard_map/hqk,khd->hqd/dot_general | solution.py:158
  199.9 19.3 %reduce-scatter.2.cloned.1.call-done = bf16[192,1536]{1,0:T(8,128)(2,1)} async-done(((bf16[192,3072]{1,0:T(8,128)(2,1)}), bf16[192,1536]{1,0:T(8,128)(2,1)}) %reduce-scatter.2.cloned.1.call-update) | async-done | bytes 589840 | tf_op jit(solution)/shard_map/reduce_scatter | solution.py:166
  (109 shorter events, 52.9 us)
Async XLA Ops:
  6.5 153.0 %all-gather.2.cloned.1.call-start = ((), (), s32[]{:S(2)}) async-start(), calls=%async_computation.1 | async-start | bytes 5222400 | tf_op jit(solution)/shard_map/all_gather | solution.py:127
  6.5 10.1 %collective-permute-start = (bf16[2,128,192]{1,2,0:T(8,128)(2,1)}, bf16[2,128,192]{1,2,0:T(8,128)(2,1)S(1)}, u32[]{:S(2)}, u32[]{:S(2)}) collective-permute-start(bf16[2,128,192]{1,2,0:T(8,128)(2,1)} %param.18), channel_id=1, source_target_pairs={{0,1},{1,2},{2,3},{3,4},{4,5},{5,6},{6,7},{7,8},{8,9},{9,10},{10,1... | collective-permute-start | bytes 294920 | tf_op jit(solution)/shard_map/ppermute | solution.py:20
  30.5 53.0 %copy-start.9 = (s32[16]{0:T(128)S(1)}, s32[16]{0:T(128)}, u32[]{:S(2)}) copy-start(s32[16]{0:T(128)} %param.26) | copy-start | bytes 196
  31.4 187.8 %reduce-scatter.2.cloned.1.call-start = ((), (), s32[]{:S(2)}) async-start(), calls=%async_computation.2 | async-start | bytes 1769472 | tf_op jit(solution)/shard_map/reduce_scatter | solution.py:166
  34.9 77.9 %copy-start.10 = (f32[128]{0:T(128)S(1)}, f32[128]{0:T(128)}, u32[]{:S(2)}) copy-start(f32[128]{0:T(128)} %param.33) | copy-start | bytes 1540
  34.9 9.0 %collective-permute-start.1 = (bf16[200,768]{1,0:T(8,128)(2,1)S(1)}, bf16[200,768]{1,0:T(8,128)(2,1)S(1)}, u32[]{:S(2)}, u32[]{:S(2)}) collective-permute-start(bf16[200,768]{1,0:T(8,128)(2,1)S(1)} %convolution_convert_fusion.1), channel_id=1, source_target_pairs={{0,1},{1,2},{2,3},{3,4},{4,5},{5,6},{6,7},{7,8},{8,9},{9,10},{10,1... | collective-permute-start | bytes 921608 | tf_op jit(solution)/shard_map/ppermute | solution.py:134
  44.0 15.7 %collective-permute-start.2 = (bf16[200,768]{1,0:T(8,128)(2,1)S(1)}, bf16[200,768]{1,0:T(8,128)(2,1)S(1)}, u32[]{:S(2)}, u32[]{:S(2)}) collective-permute-start(bf16[200,768]{1,0:T(8,128)(2,1)S(1)} %collective-permute-done.1), channel_id=1, source_target_pairs={{0,1},{1,2},{2,3},{3,4},{4,5},{5,6},{6,7},{7,8},{8,9},{9,10},{10,1... | collective-permute-start | bytes 921608 | tf_op jit(solution)/shard_map/ppermute | solution.py:134
  44.0 15.7 %collective-permute-start.9 = (bf16[200,768]{1,0:T(8,128)(2,1)S(1)}, bf16[200,768]{1,0:T(8,128)(2,1)S(1)}, u32[]{:S(2)}, u32[]{:S(2)}) collective-permute-start(bf16[200,768]{1,0:T(8,128)(2,1)S(1)} %convolution_convert_fusion.1), channel_id=1, source_target_pairs={{1,0},{2,1},{3,2},{4,3},{5,4},{6,5},{7,6},{8,7},{9,8},{10,9},{11,1... | collective-permute-start | bytes 921608 | tf_op jit(solution)/shard_map/ppermute | solution.py:136
  59.7 10.1 %collective-permute-start.3 = (bf16[200,768]{1,0:T(8,128)(2,1)S(1)}, bf16[200,768]{1,0:T(8,128)(2,1)S(1)}, u32[]{:S(2)}, u32[]{:S(2)}) collective-permute-start(bf16[200,768]{1,0:T(8,128)(2,1)S(1)} %collective-permute-done.2), channel_id=1, source_target_pairs={{0,1},{1,2},{2,3},{3,4},{4,5},{5,6},{6,7},{7,8},{8,9},{9,10},{10,1... | collective-permute-start | bytes 921608 | tf_op jit(solution)/shard_map/ppermute | solution.py:134
  59.7 15.2 %collective-permute-start.10 = (bf16[200,768]{1,0:T(8,128)(2,1)S(1)}, bf16[200,768]{1,0:T(8,128)(2,1)S(1)}, u32[]{:S(2)}, u32[]{:S(2)}) collective-permute-start(bf16[200,768]{1,0:T(8,128)(2,1)S(1)} %collective-permute-done.9), channel_id=1, source_target_pairs={{1,0},{2,1},{3,2},{4,3},{5,4},{6,5},{7,6},{8,7},{9,8},{10,9},{11,1... | collective-permute-start | bytes 921608 | tf_op jit(solution)/shard_map/ppermute | solution.py:136
  69.8 33.5 %copy-start.4 = (bf16[200,768]{1,0:T(8,128)(2,1)}, bf16[200,768]{1,0:T(8,128)(2,1)S(1)}, u32[]{:S(2)}) copy-start(bf16[200,768]{1,0:T(8,128)(2,1)S(1)} %collective-permute-done.3) | copy-start | bytes 921604
  69.8 13.7 %collective-permute-start.4 = (bf16[200,768]{1,0:T(8,128)(2,1)S(1)}, bf16[200,768]{1,0:T(8,128)(2,1)}, u32[]{:S(2)}, u32[]{:S(2)}) collective-permute-start(bf16[200,768]{1,0:T(8,128)(2,1)S(1)} %collective-permute-done.3), channel_id=1, source_target_pairs={{0,1},{1,2},{2,3},{3,4},{4,5},{5,6},{6,7},{7,8},{8,9},{9,10},{10,1... | collective-permute-start | bytes 921608 | tf_op jit(solution)/shard_map/ppermute | solution.py:134
  74.9 31.9 %copy-start.2 = (bf16[200,768]{1,0:T(8,128)(2,1)}, bf16[200,768]{1,0:T(8,128)(2,1)S(1)}, u32[]{:S(2)}) copy-start(bf16[200,768]{1,0:T(8,128)(2,1)S(1)} %collective-permute-done.10) | copy-start | bytes 921604
  74.9 10.6 %collective-permute-start.11 = (bf16[200,768]{1,0:T(8,128)(2,1)S(1)}, bf16[200,768]{1,0:T(8,128)(2,1)S(1)}, u32[]{:S(2)}, u32[]{:S(2)}) collective-permute-start(bf16[200,768]{1,0:T(8,128)(2,1)S(1)} %collective-permute-done.10), channel_id=1, source_target_pairs={{1,0},{2,1},{3,2},{4,3},{5,4},{6,5},{7,6},{8,7},{9,8},{10,9},{11,1... | collective-permute-start | bytes 921608 | tf_op jit(solution)/shard_map/ppermute | solution.py:136
  83.4 9.3 %collective-permute-start.5 = (bf16[200,768]{1,0:T(8,128)(2,1)}, bf16[200,768]{1,0:T(8,128)(2,1)S(1)}, u32[]{:S(2)}, u32[]{:S(2)}) collective-permute-start(bf16[200,768]{1,0:T(8,128)(2,1)} %collective-permute-done.4), channel_id=1, source_target_pairs={{0,1},{1,2},{2,3},{3,4},{4,5},{5,6},{6,7},{7,8},{8,9},{9,10},{10,1... | collective-permute-start | bytes 921608 | tf_op jit(solution)/shard_map/ppermute | solution.py:134
  85.5 9.0 %collective-permute-start.12 = (bf16[200,768]{1,0:T(8,128)(2,1)S(1)}, bf16[200,768]{1,0:T(8,128)(2,1)}, u32[]{:S(2)}, u32[]{:S(2)}) collective-permute-start(bf16[200,768]{1,0:T(8,128)(2,1)S(1)} %collective-permute-done.11), channel_id=1, source_target_pairs={{1,0},{2,1},{3,2},{4,3},{5,4},{6,5},{7,6},{8,7},{9,8},{10,9},{11,1... | collective-permute-start | bytes 921608 | tf_op jit(solution)/shard_map/ppermute | solution.py:136
  92.7 10.5 %collective-permute-start.6 = (bf16[200,768]{1,0:T(8,128)(2,1)S(1)}, bf16[200,768]{1,0:T(8,128)(2,1)}, u32[]{:S(2)}, u32[]{:S(2)}) collective-permute-start(bf16[200,768]{1,0:T(8,128)(2,1)S(1)} %collective-permute-done.5), channel_id=1, source_target_pairs={{0,1},{1,2},{2,3},{3,4},{4,5},{5,6},{6,7},{7,8},{8,9},{9,10},{10,1... | collective-permute-start | bytes 921608 | tf_op jit(solution)/shard_map/ppermute | solution.py:134
  94.5 12.7 %collective-permute-start.13 = (bf16[200,768]{1,0:T(8,128)(2,1)}, bf16[200,768]{1,0:T(8,128)(2,1)}, u32[]{:S(2)}, u32[]{:S(2)}) collective-permute-start(bf16[200,768]{1,0:T(8,128)(2,1)} %collective-permute-done.12), channel_id=1, source_target_pairs={{1,0},{2,1},{3,2},{4,3},{5,4},{6,5},{7,6},{8,7},{9,8},{10,9},{11,1... | collective-permute-start | bytes 921608 | tf_op jit(solution)/shard_map/ppermute | solution.py:136
  103.3 9.4 %collective-permute-start.7 = (bf16[200,768]{1,0:T(8,128)(2,1)}, bf16[200,768]{1,0:T(8,128)(2,1)}, u32[]{:S(2)}, u32[]{:S(2)}) collective-permute-start(bf16[200,768]{1,0:T(8,128)(2,1)} %collective-permute-done.6), channel_id=1, source_target_pairs={{0,1},{1,2},{2,3},{3,4},{4,5},{5,6},{6,7},{7,8},{8,9},{9,10},{10,1... | collective-permute-start | bytes 921608 | tf_op jit(solution)/shard_map/ppermute | solution.py:134
  106.9 27.5 %copy-start.3 = (bf16[200,768]{1,0:T(8,128)(2,1)S(1)}, bf16[200,768]{1,0:T(8,128)(2,1)}, u32[]{:S(2)}) copy-start(bf16[200,768]{1,0:T(8,128)(2,1)} %copy-done.2) | copy-start | bytes 921604
  107.3 9.1 %collective-permute-start.14 = (bf16[200,768]{1,0:T(8,128)(2,1)}, bf16[200,768]{1,0:T(8,128)(2,1)}, u32[]{:S(2)}, u32[]{:S(2)}) collective-permute-start(bf16[200,768]{1,0:T(8,128)(2,1)} %collective-permute-done.13), channel_id=1, source_target_pairs={{1,0},{2,1},{3,2},{4,3},{5,4},{6,5},{7,6},{8,7},{9,8},{10,9},{11,1... | collective-permute-start | bytes 921608 | tf_op jit(solution)/shard_map/ppermute | solution.py:136
  112.7 9.4 %collective-permute-start.8 = (bf16[200,768]{1,0:T(8,128)(2,1)}, bf16[200,768]{1,0:T(8,128)(2,1)}, u32[]{:S(2)}, u32[]{:S(2)}) collective-permute-start(bf16[200,768]{1,0:T(8,128)(2,1)} %collective-permute-done.7), channel_id=1, source_target_pairs={{0,1},{1,2},{2,3},{3,4},{4,5},{5,6},{6,7},{7,8},{8,9},{9,10},{10,1... | collective-permute-start | bytes 921608 | tf_op jit(solution)/shard_map/ppermute | solution.py:134
  116.4 25.6 %collective-permute-start.15 = (bf16[200,768]{1,0:T(8,128)(2,1)}, bf16[200,768]{1,0:T(8,128)(2,1)S(1)}, u32[]{:S(2)}, u32[]{:S(2)}) collective-permute-start(bf16[200,768]{1,0:T(8,128)(2,1)} %collective-permute-done.14), channel_id=1, source_target_pairs={{1,0},{2,1},{3,2},{4,3},{5,4},{6,5},{7,6},{8,7},{9,8},{10,9},{11,1... | collective-permute-start | bytes 921608 | tf_op jit(solution)/shard_map/ppermute | solution.py:136
  186.3 32.8 %copy-start.1 = (bf16[64,3072]{1,0:T(8,128)(2,1)S(1)}, bf16[64,3072]{1,0:T(8,128)(2,1)}, u32[]{:S(2)}) copy-start(bf16[64,3072]{1,0:T(8,128)(2,1)} %param.27) | copy-start | bytes 1179652
  (8 other events, 122.2 us)
Sparse Core Ops, SparseCore 0:
  31.5 71.5 all-gather.1
  200.0 19.1 reduce-scatter.1
